TPU v7x, 512 devices: a whole 4x8x8 slice. The times are simulated.
512 devices in a mesh: gx: 16 (over y, z_hi), gy: 32 (over x, z_lo, core).
Axes of the slice: x: 4, y: 8, z: 8 (z_hi: 2, z_lo: 4; z = z_hi * 4 + z_lo), core: 2. Of those that a mesh axis runs over, the one named last changes fastest.
Arguments:
- e_field: float32 [3, 8, 2048, 2048], P(None, None, 'gy', 'gx'), may hold values from -7 to 7
- h_field: float32 [3, 8, 2048, 2048], P(None, None, 'gy', 'gx'), may hold values from -7 to 7
- material: int32 [8, 2048, 2048], P(None, 'gy', 'gx'), may hold values from 0 to 7
- permittivity: float32 [8], replicated, may hold values from 1 to 12
- conductivity: float32 [8], replicated, may hold values from 0.01 to 2
- wire_layers: int32 [8], replicated, may hold values from 0 to 1, as said below
Outputs:
- e_next: float32 [3, 8, 2048, 2048], P(None, None, 'gy', 'gx')
- h_next: float32 [3, 8, 2048, 2048], P(None, None, 'gy', 'gx')
Inputs may be any that keep to these rules, and one draw needn't show every extreme that they name: `wire_layers`: exactly 4 entries are 1.
All inputs are finite; a program needn't handle non-finite values.
Results may differ from a plain program's by a relative error of at most 0.0004.
The roundings to bfloat16 on the way count: a program that leaves them out, or rounds other values in their place, can miss the bound.
Values may be sent and summed in bfloat16 or wider, within the bound.
A program may use at most 128 MiB of HBM per device.

v0:
```python
import math
import jax
import jax.numpy as jnp
from jax import lax
from jax.sharding import PartitionSpec as P

TIME_STEP = 0.9


def shifted(value, axis, steps):
    count = lax.axis_size(axis)
    pairs = [(source, (source + steps) % count) for source in range(count)]
    return lax.ppermute(value, axis, pairs)


def passed_along(shard, axis, by):
    devices = lax.axis_size(axis)
    pairs = [(i, i + by) for i in range(devices) if 0 <= i + by < devices]
    return lax.ppermute(shard, axis, pairs)


def filter_rows(first_idx, n_rows, n_cols):
    row_pos = first_idx + jnp.arange(n_rows, dtype=jnp.int32)
    col_pos = jnp.arange(n_cols, dtype=jnp.int32)
    delta = row_pos[:, None] - col_pos[None, :]
    modes = 2 * (n_cols // 4) + 1
    turned = jnp.mod(modes * delta, 2 * n_cols)
    safe_delta = jnp.where(delta == 0, 1, delta)
    upper = jnp.sin(math.pi * turned.astype(jnp.float32) / n_cols)
    lower = n_cols * jnp.sin(math.pi * safe_delta.astype(jnp.float32) / n_cols)
    band = jnp.where(delta == 0, modes / n_cols, upper / lower)
    return (0.7 * band + jnp.where(delta == 0, 0.3, 0.0)).astype(jnp.bfloat16)


def face_x(planes, direction):
    return shifted(planes, "gx", direction)


def face_y(planes, direction):
    return passed_along(planes, "gy", direction)


def ahead_z(comp):
    zeros = jnp.zeros_like(comp[:1])
    return jnp.concatenate([comp[1:], zeros], axis=0) - comp


def behind_z(comp):
    zeros = jnp.zeros_like(comp[:1])
    return comp - jnp.concatenate([zeros, comp[:-1]], axis=0)


def ahead_x(comp, edge_col):
    return jnp.concatenate([comp[:, :, 1:], edge_col[:, :, None]], axis=2) - comp


def behind_x(comp, edge_col):
    return comp - jnp.concatenate([edge_col[:, :, None], comp[:, :, :-1]], axis=2)


def ahead_y(comp, edge_row):
    return jnp.concatenate([comp[:, 1:, :], edge_row[:, None, :]], axis=1) - comp


def behind_y(comp, edge_row):
    return comp - jnp.concatenate([edge_row[:, None, :], comp[:, :-1, :]], axis=1)


def curl_of_e(e_field):
    next_x = face_x(e_field[1:3, :, :, 0], -1)
    next_y = face_y(jnp.stack([e_field[0, :, 0, :], e_field[2, :, 0, :]]), -1)
    e_x, e_y, e_z = (e_field[0], e_field[1], e_field[2])
    curl_x = ahead_y(e_z, next_y[1]) - ahead_z(e_y)
    curl_y = ahead_z(e_x) - ahead_x(e_z, next_x[1])
    curl_z = ahead_x(e_y, next_x[0]) - ahead_y(e_x, next_y[0])
    return jnp.stack([curl_x, curl_y, curl_z])


def curl_of_h(h_field):
    last_col = h_field.shape[3] - 1
    last_row = h_field.shape[2] - 1
    prev_x = face_x(h_field[1:3, :, :, last_col], 1)
    prev_y = face_y(jnp.stack([h_field[0, :, last_row, :], h_field[2, :, last_row, :]]), 1)
    h_x, h_y, h_z = (h_field[0], h_field[1], h_field[2])
    curl_x = behind_y(h_z, prev_y[1]) - behind_z(h_y)
    curl_y = behind_z(h_x) - behind_x(h_z, prev_x[1])
    curl_z = behind_x(h_y, prev_x[0]) - behind_y(h_x, prev_y[0])
    return jnp.stack([curl_x, curl_y, curl_z])


def smooth(field_in, wire_layers):
    block_rows = field_in.shape[2]
    n_layers = field_in.shape[1]
    n_wires = n_layers // 2
    n_lines = block_rows * lax.axis_size("gy")
    rank = jnp.cumsum(wire_layers) - 1
    slots = jnp.arange(n_wires, dtype=jnp.int32)
    picked = (wire_layers[None] == 1) & (rank[None] == slots[:, None])
    layer_of = jnp.sum(jnp.where(picked, jnp.arange(n_layers, dtype=jnp.int32)[None], 0), axis=1)
    wires = jnp.concatenate(
        [lax.dynamic_slice_in_dim(field_in, layer_of[k], 1, axis=1) for k in range(n_wires)], axis=1
    )
    rounded = wires.astype(jnp.bfloat16)
    f_rows = filter_rows(lax.axis_index("gy") * block_rows, block_rows, n_lines)
    filtered = jnp.einsum(
        "mn,cznx->czmx",
        f_rows,
        lax.all_gather(rounded, "gy", axis=2, tiled=True),
        preferred_element_type=jnp.float32,
    )
    out = field_in
    for k in range(n_wires):
        out = lax.dynamic_update_slice_in_dim(out, filtered[:, k : k + 1], layer_of[k], axis=1)
    return out


def body(e_field, h_field, material, permittivity, conductivity, wire_layers):
    h_half = h_field - TIME_STEP * curl_of_e(e_field)
    h_next = smooth(h_half, wire_layers)
    ratio_tab = conductivity * TIME_STEP / (2.0 * permittivity)
    decay_tab = (1.0 - ratio_tab) / (1.0 + ratio_tab)
    gain_tab = TIME_STEP / permittivity / (1.0 + ratio_tab)
    labels = jnp.arange(permittivity.shape[0], dtype=jnp.int32)
    onehot = (material[None] == labels[:, None, None, None]).astype(jnp.float32)
    decay = jnp.sum(onehot * decay_tab[:, None, None, None], axis=0)
    gain = jnp.sum(onehot * gain_tab[:, None, None, None], axis=0)
    e_half = decay[None] * e_field + gain[None] * curl_of_h(h_next)
    e_next = smooth(e_half, wire_layers)
    return (e_next, h_next)


def solution(mesh):
    placed = (
        P(None, None, "gy", "gx"),
        P(None, None, "gy", "gx"),
        P(None, "gy", "gx"),
        P(),
        P(),
        P(),
    )
    return jax.shard_map(
        body,
        mesh=mesh,
        in_specs=placed,
        out_specs=(P(None, None, "gy", "gx"), P(None, None, "gy", "gx")),
        check_vma=False,
    )
```

profile of v0, /device:TPU:1, one launch (start us, length us, event | category | flops | bytes accessed | tf_op | source)
XLA Modules:
  0.0 211.4 jit_solution(1662647163732602079)
XLA Ops:
  7.2 0.0 copy-start.1
  7.2 0.0 copy-start.3
  7.2 0.0 all-gather.3.cloned.1.call-start
  7.2 0.9 fusion.58
  8.1 8.7 %collective-permute-start = (f32[2,8,128]{2,1,0:T(8,128)S(1)}, f32[2,8,128]{2,1,0:T(8,128)S(1)}, u32[]{:S(2)}, u32[]{:S(2)}) collective-permute-start(f32[2,8,128]{2,1,0:T(8,128)S(1)} %pad_maximum_fusion.2), channel_id=1, source_target_pairs={{1,0},{2,1},{3,2},{4,3},{5,4},{6,5},{7,6},{8,7},{9,8},{10,9},{11,1... | collective-permute-start | bytes 24584 | tf_op jit(solution)/shard_map/ppermute | solution.py:19
  16.9 1.1 slice.172
  18.0 0.2 copy.62
  18.2 0.0 copy-start.5
  18.2 0.0 copy-start.6
  18.2 0.0 copy-start.4
  18.2 8.3 %collective-permute-start.1 = (f32[2,8,64]{2,1,0:T(8,128)S(1)}, f32[2,8,64]{2,1,0:T(8,128)S(1)}, u32[]{:S(2)}, u32[]{:S(2)}) collective-permute-start(f32[2,8,64]{2,1,0:T(8,128)S(1)} %bitcast.112), channel_id=1, source_target_pairs={{0,480},{32,0},{64,32},{96,64},{128,96},{160,128},{192,160},{224,1... | collective-permute-start | bytes 12296 | tf_op jit(solution)/shard_map/ppermute | solution.py:13
  26.5 1.1 slice_bitcast_fusion.13
  27.6 1.1 slice_bitcast_fusion.8
  28.7 0.7 broadcast_compare_fusion
  29.3 0.8 reduce-window.8
  30.2 0.1 slice_bitcast_fusion.4
  30.3 0.1 select_reduce_fusion.2
  30.4 0.6 fusion.61
  38.7 0.0 collective-permute-done.1
  38.7 0.1 copy.52
  38.9 0.2 copy.53
  39.0 0.0 collective-permute-done
  39.1 1.3 slice_bitcast_fusion.5
  40.3 0.1 slice.210
  40.5 0.0 copy-done.1
  40.5 0.2 fusion.17
  40.7 0.0 copy-done.3
  40.8 0.1 fusion
  40.9 0.7 pad_maximum_fusion
  41.6 0.0 all-gather.3.cloned.1.call-update
  41.7 0.0 all-gather.5.cloned.1.call-start
  41.7 0.0 copy-done.5
  41.7 0.0 copy-done.6
  41.8 0.0 copy-done.4
  41.8 0.4 select_reduce_fusion.1
  42.2 64.1 %all-gather.3.cloned.1.call-done = bf16[3,4,2048,128]{3,2,1,0:T(8,128)(2,1)} async-done(((bf16[3,4,64,128]{3,2,1,0:T(8,128)(2,1)}), bf16[3,4,2048,128]{3,2,1,0:T(8,128)(2,1)}) %all-gather.3.cloned.1.call-update) | async-done | bytes 6291472 | tf_op jit(solution)/shard_map/all_gather | solution.py:108
  106.3 6.9 %convolution_bitcast_fusion.1 = f32[3,4,64,128]{3,2,1,0:T(8,128)S(1)} fusion(bf16[3,4,2048,128]{3,2,1,0:T(8,128)(2,1)} %all-gather.3.cloned.1.call-done, s32[64]{0:T(128)S(1)} %iota_add_fusion), kind=kOutput, calls=%fused_computation.4 | convolution fusion | flops 406061056 | bytes 6684928 | tf_op jit(solution)/shard_map/mn,cznx->czmx/dot_general | solution.py:105
  113.2 0.0 copy-start
  113.3 0.4 slice_reduce_fusion
  113.7 0.7 slice_bitcast_fusion.11
  114.4 3.2 %collective-permute-start.2 = (f32[2,8,128]{2,1,0:T(8,128)S(1)}, f32[2,8,128]{2,1,0:T(8,128)S(1)}, u32[]{:S(2)}, u32[]{:S(2)}) collective-permute-start(f32[2,8,128]{2,1,0:T(8,128)S(1)} %pad_maximum_fusion.3), channel_id=1, source_target_pairs={{0,1},{1,2},{2,3},{3,4},{4,5},{5,6},{6,7},{7,8},{8,9},{9,10},{10,1... | collective-permute-start | bytes 24584 | tf_op jit(solution)/shard_map/ppermute | solution.py:19
  117.6 5.7 %collective-permute-start.3 = (f32[2,8,64]{2,1,0:T(8,128)S(1)}, f32[2,8,64]{2,1,0:T(8,128)S(1)}, u32[]{:S(2)}, u32[]{:S(2)}) collective-permute-start(f32[2,8,64]{2,1,0:T(8,128)S(1)} %slice_reduce_fusion), channel_id=1, source_target_pairs={{0,32},{32,64},{64,96},{96,128},{128,160},{160,192},{192,224},{224... | collective-permute-start | bytes 12296 | tf_op jit(solution)/shard_map/ppermute | solution.py:13
  123.4 4.7 %collective-permute-done.3 = f32[2,8,64]{2,1,0:T(8,128)S(1)} collective-permute-done((f32[2,8,64]{2,1,0:T(8,128)S(1)}, f32[2,8,64]{2,1,0:T(8,128)S(1)}, u32[]{:S(2)}, u32[]{:S(2)}) %collective-permute-start.3) | collective-permute-done | bytes 4128 | tf_op jit(solution)/shard_map/ppermute | solution.py:13
  128.0 0.2 copy.57
  128.2 0.2 copy.58
  128.4 0.0 collective-permute-done.2
  128.4 0.2 slice_bitcast_fusion.2
  128.6 1.1 fusion.22
  129.7 0.2 fusion.1
  129.9 0.7 pad_maximum_fusion.1
  130.6 0.0 all-gather.5.cloned.1.call-update
  130.6 0.0 copy-done
  130.6 66.0 %all-gather.5.cloned.1.call-done = bf16[3,4,2048,128]{3,2,1,0:T(8,128)(2,1)} async-done(((bf16[3,4,64,128]{3,2,1,0:T(8,128)(2,1)}), bf16[3,4,2048,128]{3,2,1,0:T(8,128)(2,1)}) %all-gather.5.cloned.1.call-update) | async-done | bytes 6291472 | tf_op jit(solution)/shard_map/all_gather | solution.py:108
  196.7 6.9 %convolution_bitcast_fusion = f32[3,4,64,128]{3,2,1,0:T(8,128)S(1)} fusion(bf16[3,4,2048,128]{3,2,1,0:T(8,128)(2,1)} %all-gather.5.cloned.1.call-done, s32[64]{0:T(128)S(1)} %iota_add_fusion), kind=kOutput, calls=%fused_computation.3 | convolution fusion | flops 406061056 | bytes 6684928 | tf_op jit(solution)/shard_map/mn,cznx->czmx/dot_general | solution.py:105
  203.6 0.0 copy-start.2
  203.6 0.9 copy-done.2
  (26 shorter events, 0.4 us)
Async XLA Ops:
  7.2 33.3 %copy-start.1 = (f32[3,8,64,128]{3,2,1,0:T(8,128)S(1)}, f32[3,8,64,128]{3,2,1,0:T(8,128)}, u32[]{:S(2)}) copy-start(f32[3,8,64,128]{3,2,1,0:T(8,128)} %param.6) | copy-start | bytes 2359300
  7.2 33.6 %copy-start.3 = (f32[3,8,64,128]{3,2,1,0:T(8,128)S(1)}, f32[3,8,64,128]{3,2,1,0:T(8,128)}, u32[]{:S(2)}) copy-start(f32[3,8,64,128]{3,2,1,0:T(8,128)} %param.7) | copy-start | bytes 2359300
  7.2 99.1 %all-gather.3.cloned.1.call-start = ((), (), s32[]{:S(2)}) async-start(), calls=%async_computation | async-start | bytes 6488064 | tf_op jit(solution)/shard_map/all_gather | solution.py:108
  8.1 30.9 %collective-permute-start = (f32[2,8,128]{2,1,0:T(8,128)S(1)}, f32[2,8,128]{2,1,0:T(8,128)S(1)}, u32[]{:S(2)}, u32[]{:S(2)}) collective-permute-start(f32[2,8,128]{2,1,0:T(8,128)S(1)} %pad_maximum_fusion.2), channel_id=1, source_target_pairs={{1,0},{2,1},{3,2},{4,3},{5,4},{6,5},{7,6},{8,7},{9,8},{10,9},{11,1... | collective-permute-start | bytes 24584 | tf_op jit(solution)/shard_map/ppermute | solution.py:19
  18.2 23.6 %copy-start.5 = (f32[8]{0:T(128)S(1)}, f32[8]{0:T(128)}, u32[]{:S(2)}) copy-start(f32[8]{0:T(128)} %param.9) | copy-start | bytes 100
  18.2 23.6 %copy-start.6 = (f32[8]{0:T(128)S(1)}, f32[8]{0:T(128)}, u32[]{:S(2)}) copy-start(f32[8]{0:T(128)} %param.10) | copy-start | bytes 100
  18.2 23.6 %copy-start.4 = (s32[8,64,128]{2,1,0:T(8,128)S(1)}, s32[8,64,128]{2,1,0:T(8,128)}, u32[]{:S(2)}) copy-start(s32[8,64,128]{2,1,0:T(8,128)} %param.8) | copy-start | bytes 786436
  18.2 20.5 %collective-permute-start.1 = (f32[2,8,64]{2,1,0:T(8,128)S(1)}, f32[2,8,64]{2,1,0:T(8,128)S(1)}, u32[]{:S(2)}, u32[]{:S(2)}) collective-permute-start(f32[2,8,64]{2,1,0:T(8,128)S(1)} %bitcast.112), channel_id=1, source_target_pairs={{0,480},{32,0},{64,32},{96,64},{128,96},{160,128},{192,160},{224,1... | collective-permute-start | bytes 12296 | tf_op jit(solution)/shard_map/ppermute | solution.py:13
  41.7 155.0 %all-gather.5.cloned.1.call-start = ((), (), s32[]{:S(2)}) async-start(), calls=%async_computation.1 | async-start | bytes 6488064 | tf_op jit(solution)/shard_map/all_gather | solution.py:108
  113.2 17.4 %copy-start = (f32[3,8,64,128]{3,2,1,0:T(8,128)}, f32[3,8,64,128]{3,2,1,0:T(8,128)S(1)}, u32[]{:S(2)}) copy-start(f32[3,8,64,128]{3,2,1,0:T(8,128)S(1)} %slice_dynamic-update-slice_fusion.4) | copy-start | bytes 2359300
  114.4 13.9 %collective-permute-start.2 = (f32[2,8,128]{2,1,0:T(8,128)S(1)}, f32[2,8,128]{2,1,0:T(8,128)S(1)}, u32[]{:S(2)}, u32[]{:S(2)}) collective-permute-start(f32[2,8,128]{2,1,0:T(8,128)S(1)} %pad_maximum_fusion.3), channel_id=1, source_target_pairs={{0,1},{1,2},{2,3},{3,4},{4,5},{5,6},{6,7},{7,8},{8,9},{9,10},{10,1... | collective-permute-start | bytes 24584 | tf_op jit(solution)/shard_map/ppermute | solution.py:19
  117.6 10.4 %collective-permute-start.3 = (f32[2,8,64]{2,1,0:T(8,128)S(1)}, f32[2,8,64]{2,1,0:T(8,128)S(1)}, u32[]{:S(2)}, u32[]{:S(2)}) collective-permute-start(f32[2,8,64]{2,1,0:T(8,128)S(1)} %slice_reduce_fusion), channel_id=1, source_target_pairs={{0,32},{32,64},{64,96},{96,128},{128,160},{160,192},{192,224},{224... | collective-permute-start | bytes 12296 | tf_op jit(solution)/shard_map/ppermute | solution.py:13
  203.6 0.9 copy-start.2
Sparse Core Ops, SparseCore 0:
  41.8 64.4 all-gather.2
  130.8 65.8 all-gather.4
where the time goes:
time: 212 us; the launch traced here: 211 us
  waiting for transfers between devices  135 us (64%)
  starting transfers between devices  26 us (12%)
  between operations  22.1 us (10%)
  matrix products  13.7 us (6%)
  local copies, waits for them, and re-layouts  8.13 us (4%)
  other arithmetic  6.55 us (3%)
    all_gather x2, waiting for transfers between devices, smooth(): lax.all_gather(rounded, 'gy', axis=2, tiled=True)  130 us
    ppermute x2, starting transfers between devices, shifted(): return lax.ppermute(value, axis, pairs)  14 us
    dot_general x2, matrix products, smooth(): jnp.einsum('mn,cznx->czmx', f_rows, lax.all_gather(rounded, 'gy', axis=2,...  13.7 us
    ppermute x2, starting transfers between devices, passed_along(): return lax.ppermute(shard, axis, pairs)  11.9 us
    ppermute x2, waiting for transfers between devices, shifted(): return lax.ppermute(value, axis, pairs)  4.69 us
  transfers between devices with their start and end apart: 6, of which 3 were waited for; matrix products, arithmetic and copies ran while one was open for 3% of the time, Pallas kernels for 0%

commit v1 on v0

--- a/solution.py
+++ b/solution.py
@@ -5,6 +5,10 @@
 from jax.sharding import PartitionSpec as P
 
 TIME_STEP = 0.9
+
+
+def _move_knots(state):
+    return jnp.concatenate(lax.all_to_all(jnp.stack([state] * lax.axis_size("gy")), "gy", 0, 0), 2)
 
 
 def shifted(value, axis, steps):
@@ -103,10 +107,7 @@
     rounded = wires.astype(jnp.bfloat16)
     f_rows = filter_rows(lax.axis_index("gy") * block_rows, block_rows, n_lines)
     filtered = jnp.einsum(
-        "mn,cznx->czmx",
-        f_rows,
-        lax.all_gather(rounded, "gy", axis=2, tiled=True),
-        preferred_element_type=jnp.float32,
+        "mn,cznx->czmx", f_rows, _move_knots(rounded), preferred_element_type=jnp.float32
     )
     out = field_in
     for k in range(n_wires):

time: 212 us -> 388 us (1.83)
  waiting for transfers between devices: 135 us -> 284 us
  local copies, waits for them, and re-layouts: 8.13 us -> 43.3 us
  between operations: 22.1 us -> 8.78 us
  starting transfers between devices: 26 us -> 36.6 us
  matrix products: 13.7 us -> 9.4 us
    all_to_all x0 -> x2, waiting for transfers between devices: none -> 277 us  [_move_knots(): lax.all_to_all(jnp.stack([state] * lax.axis_size('gy')), 'gy', 0, 0)]
    all_gather x2 -> x0, waiting for transfers between devices: 130 us -> none  [smooth(): lax.all_gather(rounded, 'gy', axis=2, tiled=True)]
    dynamic_update_slice x8, local copies, waits for them, and re-layouts: 0.11 us -> 15.5 us  [smooth(): lax.dynamic_update_slice_in_dim(out, filtered[:, k:k + 1], layer_of[k], a...]
    all_to_all x0 -> x2, starting transfers between devices: none -> 15.3 us  [_move_knots(): lax.all_to_all(jnp.stack([state] * lax.axis_size('gy')), 'gy', 0, 0)]
    another operation x2 -> x8, local copies, waits for them, and re-layouts: 0.08 us -> 9.16 us  [the longest x2 8.41 us: _move_knots(): jnp.stack([state] * lax.axis_size('gy'))]
    reshape x0 -> x2, local copies, waits for them, and re-layouts: none -> 8.56 us  [_move_knots(): jnp.concatenate(lax.all_to_all(jnp.stack([state] * lax.axis_size('gy')),...]
    ppermute x2, starting transfers between devices: 11.9 us -> 4.78 us  [passed_along(): return lax.ppermute(shard, axis, pairs)]
    dot_general x2, matrix products: 13.7 us -> 9.4 us  [smooth(): jnp.einsum('mn,cznx->czmx', f_rows, _move_knots(rounded), preferred_eleme...]
  transfers between devices with their start and end apart: 6 -> 6, of which waited for: 3 -> 3; matrix products, arithmetic and copies ran while one was open for 3% -> 2% of each run, Pallas kernels for 0% -> 0%
where the time goes in v1:
time: 388 us; the launch traced here: 387 us
  waiting for transfers between devices  284 us (73%)
  local copies, waits for them, and re-layouts  43.3 us (11%)
  starting transfers between devices  36.6 us (9%)
  matrix products  9.4 us (2%)
  between operations  8.78 us (2%)
  other arithmetic  5.63 us (1%)
    all_to_all x2, waiting for transfers between devices, _move_knots(): lax.all_to_all(jnp.stack([state] * lax.axis_size('gy')), 'gy', 0, 0)  277 us
    ppermute x2, starting transfers between devices, shifted(): return lax.ppermute(value, axis, pairs)  16.5 us
    dynamic_update_slice x8, local copies, waits for them, and re-layouts, smooth(): lax.dynamic_update_slice_in_dim(out, filtered[:, k:k + 1], layer_of[k], a...  15.5 us
    all_to_all x2, starting transfers between devices, _move_knots(): lax.all_to_all(jnp.stack([state] * lax.axis_size('gy')), 'gy', 0, 0)  15.3 us
    dot_general x2, matrix products, smooth(): jnp.einsum('mn,cznx->czmx', f_rows, _move_knots(rounded), preferred_eleme...  9.4 us
    reshape x2, local copies, waits for them, and re-layouts, _move_knots(): jnp.concatenate(lax.all_to_all(jnp.stack([state] * lax.axis_size('gy')),...  8.56 us
    another operation x2, local copies, waits for them, and re-layouts, _move_knots(): jnp.stack([state] * lax.axis_size('gy'))  8.41 us
  transfers between devices with their start and end apart: 6, of which 3 were waited for; matrix products, arithmetic and copies ran while one was open for 2% of the time, Pallas kernels for 0%

profile of v1, /device:TPU:1, one launch (start us, length us, event | category | flops | bytes accessed | tf_op | source)
XLA Modules:
  0.0 387.2 jit_solution(17449883475078725413)
XLA Ops:
  0.6 0.0 copy-start.1
  0.6 1.2 slice.172
  1.8 0.2 copy.231
  2.0 14.4 %collective-permute-start.1 = (f32[2,8,64]{2,1,0:T(8,128)S(1)}, f32[2,8,64]{2,1,0:T(8,128)S(1)}, u32[]{:S(2)}, u32[]{:S(2)}) collective-permute-start(f32[2,8,64]{2,1,0:T(8,128)S(1)} %bitcast.121), channel_id=1, source_target_pairs={{0,480},{32,0},{64,32},{96,64},{128,96},{160,128},{192,160},{224,1... | collective-permute-start | bytes 12296 | tf_op jit(solution)/shard_map/ppermute | solution.py:17
  16.4 1.6 copy.200
  18.0 2.9 collective-permute-start
  21.0 0.7 broadcast_compare_fusion
  21.6 0.8 reduce-window.8
  22.5 0.1 slice_bitcast_fusion.4
  22.6 0.1 select_reduce_fusion.2
  22.7 0.7 fusion.59
  31.0 0.0 collective-permute-done.1
  31.1 0.2 copy.210
  31.2 0.2 copy.211
  31.4 0.0 collective-permute-done
  31.4 0.2 slice_bitcast_fusion.7
  31.6 0.1 slice.217
  31.8 0.2 fusion.17
  31.9 0.0 copy-done.1
  32.0 0.5 fusion
  32.5 0.4 dynamic-slice_convert_fusion.7
  32.9 0.5 pad_maximum_fusion
  33.4 4.2 %stack.24 = bf16[32,3,4,64,128]{4,3,2,1,0:T(8,128)(2,1)} broadcast(bf16[3,4,64,128]{3,2,1,0:T(8,128)(2,1)S(1)} %copy.213), dimensions={1,2,3,4} | broadcast | bytes 6488064 | tf_op jit(solution)/shard_map/stack | solution.py:11
  37.6 7.5 %all-to-all-start = ((bf16[32,3,4,64,128]{4,3,2,1,0:T(8,128)(2,1)}), bf16[32,3,4,64,128]{4,3,2,1,0:T(8,128)(2,1)}, u32[]{:S(2)}, u32[]{:S(2)}) async-start(bf16[32,3,4,64,128]{4,3,2,1,0:T(8,128)(2,1)} %stack.24), calls=%async_computation | async-start | bytes 12582912 | tf_op jit(solution)/shard_map/all_to_all | solution.py:11
  45.1 0.0 copy-done.3
  45.1 0.0 copy-done.4
  45.1 0.0 copy-done.2
  45.1 0.4 select_reduce_fusion.1
  45.6 0.2 copy.199
  45.7 0.2 copy.201
  45.9 138.6 %all-to-all-done = bf16[32,3,4,64,128]{4,3,2,1,0:T(8,128)(2,1)} async-done(((bf16[32,3,4,64,128]{4,3,2,1,0:T(8,128)(2,1)}), bf16[32,3,4,64,128]{4,3,2,1,0:T(8,128)(2,1)}, u32[]{:S(2)}, u32[]{:S(2)}) %all-to-all-start) | async-done | bytes 6291488 | tf_op jit(solution)/shard_map/all_to_all | solution.py:11
  184.5 4.3 %copy.214 = bf16[3,4,32,64,128]{4,3,2,1,0:T(8,128)(2,1)S(1)} copy(bf16[3,4,32,64,128]{4,3,1,0,2:T(8,128)(2,1)} %bitcast.22) | data formatting | bytes 12582912 | tf_op jit(solution)/shard_map/reshape | solution.py:11
  188.8 4.7 %convolution_bitcast_fusion.1 = f32[3,4,64,128]{3,2,1,0:T(8,128)S(1)} fusion(bf16[3,4,2048,128]{3,2,1,0:T(8,128)(2,1)S(1)} %bitcast.111, s32[64]{0:T(128)S(1)} %iota_add_fusion), kind=kOutput, calls=%fused_computation.4 | convolution fusion | flops 406061056 | bytes 6684928 | tf_op jit(solution)/shard_map/mn,cznx->czmx/dot_general | solution.py:109
  193.5 0.0 copy-start
  193.5 1.9 dynamic_update_slice.24
  195.5 1.9 dynamic_update_slice.25
  197.4 1.9 dynamic_update_slice.26
  199.3 1.9 dynamic_update_slice.27
  201.3 0.2 slice.236
  201.5 0.7 slice_bitcast_fusion.10
  202.3 1.9 collective-permute-start.2
  204.2 0.2 copy.219
  204.4 2.1 collective-permute-start.3
  206.6 1.7 slice_bitcast_fusion.8
  208.3 6.6 %collective-permute-done.3 = f32[2,8,64]{2,1,0:T(8,128)S(1)} collective-permute-done((f32[2,8,64]{2,1,0:T(8,128)S(1)}, f32[2,8,64]{2,1,0:T(8,128)S(1)}, u32[]{:S(2)}, u32[]{:S(2)}) %collective-permute-start.3) | collective-permute-done | bytes 4128 | tf_op jit(solution)/shard_map/ppermute | solution.py:17
  214.9 0.2 copy.220
  215.0 0.2 copy.221
  215.2 0.0 collective-permute-done.2
  215.2 1.1 slice_bitcast_fusion.3
  216.4 0.2 fusion.22
  216.5 0.5 fusion.1
  217.1 0.4 dynamic-slice_convert_fusion.3
  217.5 0.5 pad_maximum_fusion.1
  218.0 4.2 %stack.29 = bf16[32,3,4,64,128]{4,3,2,1,0:T(8,128)(2,1)} broadcast(bf16[3,4,64,128]{3,2,1,0:T(8,128)(2,1)S(1)} %copy.222), dimensions={1,2,3,4} | broadcast | bytes 6488064 | tf_op jit(solution)/shard_map/stack | solution.py:11
  222.2 7.8 %all-to-all-start.1 = ((bf16[32,3,4,64,128]{4,3,2,1,0:T(8,128)(2,1)}), bf16[32,3,4,64,128]{4,3,2,1,0:T(8,128)(2,1)}, u32[]{:S(2)}, u32[]{:S(2)}) async-start(bf16[32,3,4,64,128]{4,3,2,1,0:T(8,128)(2,1)} %stack.29), calls=%async_computation.1 | async-start | bytes 12582912 | tf_op jit(solution)/shard_map/all_to_all | solution.py:11
  230.0 1.0 copy.229
  231.0 138.4 %all-to-all-done.1 = bf16[32,3,4,64,128]{4,3,2,1,0:T(8,128)(2,1)} async-done(((bf16[32,3,4,64,128]{4,3,2,1,0:T(8,128)(2,1)}), bf16[32,3,4,64,128]{4,3,2,1,0:T(8,128)(2,1)}, u32[]{:S(2)}, u32[]{:S(2)}) %all-to-all-start.1) | async-done | bytes 6291488 | tf_op jit(solution)/shard_map/all_to_all | solution.py:11
  369.4 4.3 %copy.223 = bf16[3,4,32,64,128]{4,3,2,1,0:T(8,128)(2,1)S(1)} copy(bf16[3,4,32,64,128]{4,3,1,0,2:T(8,128)(2,1)} %bitcast.47) | data formatting | bytes 12582912 | tf_op jit(solution)/shard_map/reshape | solution.py:11
  373.7 4.7 %convolution_bitcast_fusion = f32[3,4,64,128]{3,2,1,0:T(8,128)S(1)} fusion(bf16[3,4,2048,128]{3,2,1,0:T(8,128)(2,1)S(1)} %bitcast.110, s32[64]{0:T(128)S(1)} %iota_add_fusion), kind=kOutput, calls=%fused_computation.3 | convolution fusion | flops 406061056 | bytes 6684928 | tf_op jit(solution)/shard_map/mn,cznx->czmx/dot_general | solution.py:109
  378.4 1.9 dynamic_update_slice.28
  380.3 1.9 dynamic_update_slice.29
  382.3 1.9 dynamic_update_slice.30
  384.2 1.9 dynamic_update_slice.31
  386.2 1.0 copy.228
  (27 shorter events, 0.4 us)
Async XLA Ops:
  0.6 31.3 %copy-start.1 = (f32[3,8,64,128]{3,2,1,0:T(8,128)S(1)}, f32[3,8,64,128]{3,2,1,0:T(8,128)}, u32[]{:S(2)}) copy-start(f32[3,8,64,128]{3,2,1,0:T(8,128)} %param.7) | copy-start | bytes 2359300
  2.0 29.0 %collective-permute-start.1 = (f32[2,8,64]{2,1,0:T(8,128)S(1)}, f32[2,8,64]{2,1,0:T(8,128)S(1)}, u32[]{:S(2)}, u32[]{:S(2)}) collective-permute-start(f32[2,8,64]{2,1,0:T(8,128)S(1)} %bitcast.121), channel_id=1, source_target_pairs={{0,480},{32,0},{64,32},{96,64},{128,96},{160,128},{192,160},{224,1... | collective-permute-start | bytes 12296 | tf_op jit(solution)/shard_map/ppermute | solution.py:17
  18.0 13.4 %collective-permute-start = (f32[2,8,128]{2,1,0:T(8,128)S(1)}, f32[2,8,128]{2,1,0:T(8,128)S(1)}, u32[]{:S(2)}, u32[]{:S(2)}) collective-permute-start(f32[2,8,128]{2,1,0:T(8,128)S(1)} %pad_maximum_fusion.2), channel_id=1, source_target_pairs={{1,0},{2,1},{3,2},{4,3},{5,4},{6,5},{7,6},{8,7},{9,8},{10,9},{11,1... | collective-permute-start | bytes 24584 | tf_op jit(solution)/shard_map/ppermute | solution.py:23
  37.6 7.5 %copy-start.3 = (f32[8]{0:T(128)S(1)}, f32[8]{0:T(128)}, u32[]{:S(2)}) copy-start(f32[8]{0:T(128)} %param.9) | copy-start | bytes 100
  37.6 7.5 %copy-start.4 = (f32[8]{0:T(128)S(1)}, f32[8]{0:T(128)}, u32[]{:S(2)}) copy-start(f32[8]{0:T(128)} %param.10) | copy-start | bytes 100
  37.6 7.6 %copy-start.2 = (s32[8,64,128]{2,1,0:T(8,128)S(1)}, s32[8,64,128]{2,1,0:T(8,128)}, u32[]{:S(2)}) copy-start(s32[8,64,128]{2,1,0:T(8,128)} %param.8) | copy-start | bytes 786436
  37.6 146.9 %all-to-all-start = ((bf16[32,3,4,64,128]{4,3,2,1,0:T(8,128)(2,1)}), bf16[32,3,4,64,128]{4,3,2,1,0:T(8,128)(2,1)}, u32[]{:S(2)}, u32[]{:S(2)}) async-start(bf16[32,3,4,64,128]{4,3,2,1,0:T(8,128)(2,1)} %stack.24), calls=%async_computation | async-start | bytes 12582912 | tf_op jit(solution)/shard_map/all_to_all | solution.py:11
  193.5 23.1 %copy-start = (f32[3,8,64,128]{3,2,1,0:T(8,128)S(1)}, f32[3,8,64,128]{3,2,1,0:T(8,128)}, u32[]{:S(2)}) copy-start(f32[3,8,64,128]{3,2,1,0:T(8,128)} %param.6) | copy-start | bytes 2359300
  202.3 12.9 %collective-permute-start.2 = (f32[2,8,128]{2,1,0:T(8,128)S(1)}, f32[2,8,128]{2,1,0:T(8,128)S(1)}, u32[]{:S(2)}, u32[]{:S(2)}) collective-permute-start(f32[2,8,128]{2,1,0:T(8,128)S(1)} %pad_maximum_fusion.3), channel_id=1, source_target_pairs={{0,1},{1,2},{2,3},{3,4},{4,5},{5,6},{6,7},{7,8},{8,9},{9,10},{10,1... | collective-permute-start | bytes 24584 | tf_op jit(solution)/shard_map/ppermute | solution.py:23
  204.4 10.4 %collective-permute-start.3 = (f32[2,8,64]{2,1,0:T(8,128)S(1)}, f32[2,8,64]{2,1,0:T(8,128)S(1)}, u32[]{:S(2)}, u32[]{:S(2)}) collective-permute-start(f32[2,8,64]{2,1,0:T(8,128)S(1)} %bitcast.122), channel_id=1, source_target_pairs={{0,32},{32,64},{64,96},{96,128},{128,160},{160,192},{192,224},{224... | collective-permute-start | bytes 12296 | tf_op jit(solution)/shard_map/ppermute | solution.py:17
  222.2 147.2 %all-to-all-start.1 = ((bf16[32,3,4,64,128]{4,3,2,1,0:T(8,128)(2,1)}), bf16[32,3,4,64,128]{4,3,2,1,0:T(8,128)(2,1)}, u32[]{:S(2)}, u32[]{:S(2)}) async-start(bf16[32,3,4,64,128]{4,3,2,1,0:T(8,128)(2,1)} %stack.29), calls=%async_computation.1 | async-start | bytes 12582912 | tf_op jit(solution)/shard_map/all_to_all | solution.py:11
